TPU v7x, 32 devices: a whole 2x2x4 slice. The times are simulated.
32 devices in a mesh: dp: 16 (over z, x, core), fac: 2 (over y).
Axes of the slice: x: 2, y: 2, z: 4, core: 2. Of those that a mesh axis runs over, the one named last changes fastest.
Arguments:
- occupations: int32 [32, 256], P('dp'), may hold values from 0 to 1, as said below
- stream: bfloat16 [8192, 2048], P('dp', 'fac'), may hold values from -6 to 6
- norm_gain: float32 [2048], replicated, may hold values from 0.1 to 1.9
- probs: bfloat16 [32, 16, 256, 256], P('dp', 'fac'), may hold values from 0 to 1, as said below
- w_out: bfloat16 [2048, 2048], P('fac', 'dp'), may hold values from -0.125 to 0.125
- cotangent: bfloat16 [8192, 2048], P('dp', 'fac'), may hold values from -6 to 6
Outputs:
- update: float32 [2048, 2048], P('dp', 'fac')
Inputs may be any that keep to these rules, and one draw needn't show every extreme that they name: `occupations`: each sample holds exactly 48 ones. `probs`: within each sample and head, entries with the key after the query are zero and each row sums to one up to bfloat16 rounding.
All inputs are finite; a program needn't handle non-finite values.
Results may differ from a plain program's by a relative error of at most 0.0051.
Values may be sent and summed in bfloat16 or wider, within the bound.
No kernel may reach another device: no remote copies, remote signals or barrier semaphores. Data moves between devices by JAX's collectives and lax.ppermute only.
A program may use at most 128 MiB of HBM per device.

v0:
```python
import jax
import jax.numpy as jnp
from jax import lax
from jax.sharding import PartitionSpec as P

ORBS = 256
NE = 48
damping = 0.1
epsilon = 1e-06
highest = lax.Precision.HIGHEST
contract_first = (((0,), (0,)), ((), ()))


def keep_mask(occupations):
    before = jnp.cumsum(occupations, axis=1) - occupations
    position = lax.broadcasted_iota(jnp.int32, occupations.shape, 1)
    forced = (before == NE) | (position - before == ORBS - NE)
    return 1 - forced.astype(jnp.int32)


def panel_rows(block):
    return lax.all_gather(block, "fac", axis=2, tiled=True)


def panel_product(left_rows, right_block):
    return jnp.einsum(
        "brk,bkc->brc",
        left_rows,
        lax.all_gather(right_block, "dp", axis=1, tiled=True),
        precision=highest,
    )


def per_device(occupations, stream, norm_gain, probs, w_out, cotangent):
    width = norm_gain.shape[0]
    samples = occupations.shape[0]
    tokens = samples * ORBS
    data_count = lax.axis_size("dp")
    fac_count = lax.axis_size("fac")
    block_rows = width // data_count
    block_cols = width // fac_count
    data_index = lax.axis_index("dp")
    fac_index = lax.axis_index("fac")
    scale = 1.0 / (tokens * data_count)
    stream_whole, cotangent_whole = (
        lax.all_gather(stream, "fac", axis=1, tiled=True),
        lax.all_gather(cotangent, "fac", axis=1, tiled=True),
    )
    values = stream_whole.astype(jnp.float32)
    mean_square = jnp.mean(values * values, axis=1, keepdims=True)
    normed = (values * lax.rsqrt(mean_square + epsilon) * norm_gain).astype(jnp.bfloat16)
    normed_cols = lax.dynamic_slice_in_dim(normed, fac_index * block_cols, block_cols, 1)
    keep = keep_mask(occupations).reshape(tokens, 1).astype(jnp.bfloat16)
    upstream = cotangent_whole * keep
    out_grad = lax.dot_general(
        upstream,
        lax.all_gather(w_out, "dp", axis=1, tiled=True),
        (((1,), (1,)), ((), ())),
        preferred_element_type=jnp.float32,
    ).astype(jnp.bfloat16)
    local_heads = probs.shape[1]
    head_width = block_cols // local_heads
    per_head = out_grad.reshape(samples, ORBS, local_heads, head_width)
    value_local = jnp.einsum("shij,sihe->sjhe", probs, per_head, preferred_element_type=jnp.float32)
    value_local = value_local.reshape(tokens, block_cols).astype(jnp.bfloat16)
    value_whole = lax.all_gather(value_local, "fac", axis=1, tiled=True)
    g_part = (
        lax.dot_general(
            value_whole, value_local, contract_first, preferred_element_type=jnp.float32
        )
        * scale
    )
    grad_part = (
        lax.dot_general(normed, value_local, contract_first, preferred_element_type=jnp.float32)
        * scale
    )
    a_part = (
        lax.dot_general(normed, normed_cols, contract_first, preferred_element_type=jnp.float32)
        * scale
    )
    a_block, g_block, grad_block = (
        lax.psum_scatter(a_part, "dp", scatter_dimension=0, tiled=True),
        lax.psum_scatter(g_part, "dp", scatter_dimension=0, tiled=True),
        lax.psum_scatter(grad_part, "dp", scatter_dimension=0, tiled=True),
    )
    row_ids = data_index * block_rows + lax.broadcasted_iota(jnp.int32, (block_rows, block_cols), 0)
    col_ids = fac_index * block_cols + lax.broadcasted_iota(jnp.int32, (block_rows, block_cols), 1)
    identity_block = (row_ids == col_ids).astype(jnp.float32)
    a_block = a_block + damping * identity_block
    g_block = g_block + damping * identity_block
    norm_a, norm_g = lax.psum(
        (jnp.sum(a_block * a_block), jnp.sum(g_block * g_block)), ("dp", "fac")
    )
    alphas = (1.0 / jnp.sqrt(jnp.stack([norm_a, norm_g]))).reshape(2, 1, 1)
    factors = jnp.stack([a_block, g_block])
    iterate = 2.0 * alphas * identity_block[None] - alphas * alphas * factors
    columns = lax.all_gather(iterate, "dp", axis=1, tiled=True)
    product = jnp.einsum("brk,bkc->brc", panel_rows(factors), columns, precision=highest)
    iterate = 2.0 * iterate - jnp.einsum(
        "brk,bkc->brc", panel_rows(product), columns, precision=highest
    )
    left_side = panel_product(panel_rows(iterate[0:1]), grad_block[None])
    pre = panel_product(panel_rows(left_side), iterate[1:2])[0]
    inner_sum = lax.psum(jnp.sum(grad_block * pre), ("dp", "fac"))
    return pre * (width / jnp.sqrt(inner_sum + epsilon))


def solution(mesh):
    placed = (
        P("dp", None),
        P("dp", "fac"),
        P(),
        P("dp", "fac", None, None),
        P("fac", "dp"),
        P("dp", "fac"),
    )
    return jax.shard_map(
        per_device, mesh=mesh, in_specs=placed, out_specs=P("dp", "fac"), check_vma=False
    )
```

profile of v0, /device:TPU:0, one launch (start us, length us, event | category | flops | bytes accessed | tf_op | source)
XLA Modules:
  0.0 988.1 jit_solution(5292536521925925867)
XLA Ops:
  6.5 0.7 all-gather.16.cloned.1.call-update
  7.3 0.0 all-gather.18.cloned.1.call-start
  7.3 0.7 all-gather.18.cloned.1.call-update
  8.0 0.0 all-gather.14.cloned.1.call-start
  8.1 0.7 all-gather.14.cloned.1.call-update
  8.7 0.0 all-gather.20.cloned.1.call-start
  8.8 0.7 reshape.106
  9.5 0.6 reduce-window.6
  10.1 0.2 slice_reduce_fusion
  10.3 0.2 reduce-window.9
  10.5 0.1 add_bitcast_fusion
  10.6 0.7 fusion.23
  11.3 33.5 %all-gather.16.cloned.1.call-done = bf16[512,2048]{1,0:T(8,128)(2,1)} async-done(((bf16[512,1024]{1,0:T(8,128)(2,1)}), bf16[512,2048]{1,0:T(8,128)(2,1)}) %all-gather.16.cloned.1.call-update) | async-done | bytes 2097168 | tf_op jit(solution)/shard_map/all_gather | solution.py:47
  44.7 54.7 %all-gather.18.cloned.1.call-done = bf16[1024,2048]{1,0:T(8,128)(2,1)} async-done(((bf16[1024,128]{1,0:T(8,128)(2,1)}), bf16[1024,2048]{1,0:T(8,128)(2,1)}) %all-gather.18.cloned.1.call-update) | async-done | bytes 4194320 | tf_op jit(solution)/shard_map/all_gather | solution.py:57
  99.4 5.2 fusion.11
  104.6 0.3 copy.12
  104.9 0.5 fusion.10
  105.4 0.8 copy.9
  106.2 1.3 copy.26
  107.5 0.0 all-gather.20.cloned.1.call-update
  107.5 0.0 reduce-scatter.4.cloned.1.call-start
  107.5 24.7 %all-gather.14.cloned.1.call-done = bf16[512,2048]{1,0:T(8,128)(2,1)} async-done(((bf16[512,1024]{1,0:T(8,128)(2,1)}), bf16[512,2048]{1,0:T(8,128)(2,1)}) %all-gather.14.cloned.1.call-update) | async-done | bytes 2097168 | tf_op jit(solution)/shard_map/all_gather | solution.py:46
  132.3 2.1 fusion.2
  134.4 2.1 fusion.4
  136.5 1.3 copy-done.3
  137.8 5.8 convolution_multiply_fusion.2
  143.7 0.0 reduce-scatter.4.cloned.1.call-update
  143.7 0.0 reduce-scatter.6.cloned.1.call-start
  143.7 23.0 %all-gather.20.cloned.1.call-done = bf16[512,2048]{1,0:T(8,128)(2,1)} async-done(((bf16[512,1024]{1,0:T(8,128)(2,1)}), bf16[512,2048]{1,0:T(8,128)(2,1)}) %all-gather.20.cloned.1.call-update) | async-done | bytes 2097168 | tf_op jit(solution)/shard_map/all_gather | solution.py:66
  166.8 7.2 convolution_multiply_fusion.1
  174.0 0.0 all-gather.22.cloned.1.call-start
  174.1 0.1 compare_convert_fusion
  174.2 100.0 %reduce-scatter.4.cloned.1.call-done = f32[128,1024]{1,0:T(8,128)} async-done(((f32[2048,1024]{1,0:T(8,128)}), f32[128,1024]{1,0:T(8,128)}) %reduce-scatter.4.cloned.1.call-update) | async-done | bytes 524304 | tf_op jit(solution)/shard_map/reduce_scatter | solution.py:82
  274.1 107.1 %reduce-scatter.6.cloned.1.call-done = f32[128,1024]{1,0:T(8,128)} async-done(((f32[2048,1024]{1,0:T(8,128)}), f32[128,1024]{1,0:T(8,128)}) %reduce-scatter.6.cloned.1.call-update) | async-done | bytes 524304 | tf_op jit(solution)/shard_map/reduce_scatter | solution.py:83
  381.2 2.1 multiply_reduce_fusion.2
  383.3 40.5 %all-reduce = (f32[1]{0:T(128)}, f32[1]{0:T(128)}) all-reduce(f32[1]{0:T(128)} %bitcast.2, f32[1]{0:T(128)} %bitcast), channel_id=1, replica_groups=mesh['dp'=16,'fac'=2] {'dp','fac'}, use_global_device_ids=true, to_apply=%region_8.9 | all-reduce | flops 2 | bytes 16 | tf_op jit(solution)/shard_map/psum | solution.py:91
  423.9 1.3 broadcast_multiply_fusion.1
  425.2 1.5 multiply_subtract_fusion
  426.6 0.0 all-gather.24.cloned.1.call-start
  426.7 0.7 all-gather.24.cloned.1.call-update
  427.4 0.2 reduce-scatter.8.cloned.1.call-start
  427.6 7.5 convolution_multiply_fusion
  435.2 0.0 reduce-scatter.8.cloned.1.call-update
  435.2 0.0 all-gather.26.cloned.1.call-start
  435.3 24.2 %all-gather.22.cloned.1.call-done = f32[2,128,2048]{2,1,0:T(8,128)} async-done(((f32[2,128,1024]{2,1,0:T(8,128)}), f32[2,128,2048]{2,1,0:T(8,128)}) %all-gather.22.cloned.1.call-update) | async-done | bytes 2097168 | tf_op jit(solution)/shard_map/all_gather | solution.py:22
  459.5 128.7 %all-gather.24.cloned.1.call-done = f32[2,2048,1024]{2,1,0:T(8,128)} async-done(((f32[2,128,1024]{2,1,0:T(8,128)}), f32[2,2048,1024]{2,1,0:T(8,128)}) %all-gather.24.cloned.1.call-update) | async-done | bytes 16777232 | tf_op jit(solution)/shard_map/all_gather | solution.py:97
  588.1 14.4 %fusion.27 = f32[2,128,1024]{2,1,0:T(8,128)} fusion(f32[2,128,2048]{2,1,0:T(8,128)} %all-gather.22.cloned.1.call-done, f32[2,2048,1024]{2,1,0:T(8,128)} %all-gather.24.cloned.1.call-done), kind=kOutput, calls=%fused_computation.49 | convolution fusion | flops 6442450944 | bytes 19922944 | tf_op jit(solution)/shard_map/brk,bkc->brc/dot_general | solution.py:98
  602.5 0.0 all-gather.32.cloned.1.call-start
  602.6 91.3 %reduce-scatter.8.cloned.1.call-done = f32[128,1024]{1,0:T(8,128)} async-done(((f32[2048,1024]{1,0:T(8,128)}), f32[128,1024]{1,0:T(8,128)}) %reduce-scatter.8.cloned.1.call-update) | async-done | bytes 524304 | tf_op jit(solution)/shard_map/reduce_scatter | solution.py:84
  693.9 0.0 all-gather.28.cloned.1.call-start
  693.9 34.1 %all-gather.26.cloned.1.call-done = f32[2,128,2048]{2,1,0:T(8,128)} async-done(((f32[2,128,1024]{2,1,0:T(8,128)}), f32[2,128,2048]{2,1,0:T(8,128)}) %all-gather.26.cloned.1.call-update) | async-done | bytes 2097168 | tf_op jit(solution)/shard_map/all_gather | solution.py:22
  728.0 13.7 %convolution_subtract_fusion = f32[2,128,1024]{2,1,0:T(8,128)S(1)} fusion(f32[2,128,2048]{2,1,0:T(8,128)} %all-gather.26.cloned.1.call-done, f32[2,2048,1024]{2,1,0:T(8,128)} %all-gather.24.cloned.1.call-done, f32[2,128,1024]{2,1,0:T(8,128)S(1)} %copy-done.2), kind=kOutput, calls=%fused_computation.16 | convolution fusion | flops 6442975232 | bytes 20971520 | tf_op jit(solution)/shard_map/brk,bkc->brc/dot_general | solution.py:99
  741.7 1.1 fusion.26
  742.9 0.3 all-gather.34.cloned.1.call-start
  743.1 61.4 %all-gather.32.cloned.1.call-done = f32[2048,1024]{1,0:T(8,128)} async-done(((f32[128,1024]{1,0:T(8,128)}), f32[2048,1024]{1,0:T(8,128)}) %all-gather.32.cloned.1.call-update) | async-done | bytes 8388624 | tf_op jit(solution)/shard_map/all_gather | solution.py:29
  804.5 21.3 %all-gather.28.cloned.1.call-done = f32[1,128,2048]{2,1,0:T(8,128)} async-done(((f32[1,128,1024]{2,1,0:T(8,128)}), f32[1,128,2048]{2,1,0:T(8,128)}) %all-gather.28.cloned.1.call-update) | async-done | bytes 1048592 | tf_op jit(solution)/shard_map/all_gather | solution.py:22
  825.8 9.2 fusion.14
  835.0 0.0 all-gather.30.cloned.1.call-start
  835.0 0.5 all-gather.30.cloned.1.call-update
  835.6 20.8 %all-gather.34.cloned.1.call-done = f32[128,2048]{1,0:T(8,128)} async-done(((f32[128,1024]{1,0:T(8,128)}), f32[128,2048]{1,0:T(8,128)}) %all-gather.34.cloned.1.call-update) | async-done | bytes 1048592 | tf_op jit(solution)/shard_map/all_gather | solution.py:22
  856.4 76.3 %all-gather.30.cloned.1.call-done = f32[1,2048,1024]{2,1,0:T(8,128)} async-done(((f32[1,128,1024]{2,1,0:T(8,128)}), f32[1,2048,1024]{2,1,0:T(8,128)}) %all-gather.30.cloned.1.call-update) | async-done | bytes 8388624 | tf_op jit(solution)/shard_map/all_gather | solution.py:29
  932.8 8.2 multiply_reduce_fusion
  940.9 39.1 %psum.23 = f32[]{:T(128)} all-reduce(f32[]{:T(128)} %get-tuple-element.15), channel_id=1, replica_groups=mesh['dp'=16,'fac'=2] {'dp','fac'}, use_global_device_ids=true, to_apply=%region_11.12 | all-reduce | flops 1 | bytes 8 | tf_op jit(solution)/shard_map/psum | solution.py:104
  980.7 0.8 broadcast_multiply_fusion
  (22 shorter events, 0.1 us)
Async XLA Ops:
  6.5 98.3 %copy-start = (bf16[2,8,256,256]{3,2,1,0:T(8,128)(2,1)S(1)}, bf16[2,8,256,256]{3,2,1,0:T(8,128)(2,1)}, u32[]{:S(2)}) copy-start(bf16[2,8,256,256]{3,2,1,0:T(8,128)(2,1)} %param.9) | copy-start | bytes 6291460
  6.5 38.2 %all-gather.16.cloned.1.call-start = ((), (), s32[]{:S(2)}) async-start(), calls=%async_computation.5 | async-start | bytes 3145728 | tf_op jit(solution)/shard_map/all_gather | solution.py:47
  7.3 92.1 %all-gather.18.cloned.1.call-start = ((), (), s32[]{:S(2)}) async-start(), calls=%async_computation.6 | async-start | bytes 4456448 | tf_op jit(solution)/shard_map/all_gather | solution.py:57
  8.0 124.3 %all-gather.14.cloned.1.call-start = ((), (), s32[]{:S(2)}) async-start(), calls=%async_computation.3 | async-start | bytes 3145728 | tf_op jit(solution)/shard_map/all_gather | solution.py:46
  8.7 158.0 %all-gather.20.cloned.1.call-start = ((), (), s32[]{:S(2)}) async-start(), calls=%async_computation.7 | async-start | bytes 3145728 | tf_op jit(solution)/shard_map/all_gather | solution.py:66
  105.4 28.9 %copy-start.5 = (f32[2048]{0:T(1024)S(1)}, f32[2048]{0:T(1024)}, u32[]{:S(2)}) copy-start(f32[2048]{0:T(1024)} %param.8) | copy-start | bytes 24580
  107.5 166.7 %reduce-scatter.4.cloned.1.call-start = ((), (), s32[]{:S(2)}) async-start(), calls=%async_computation.4 | async-start | bytes 8912896 | tf_op jit(solution)/shard_map/reduce_scatter | solution.py:82
  136.5 1.3 copy-start.3
  143.7 237.5 %reduce-scatter.6.cloned.1.call-start = ((), (), s32[]{:S(2)}) async-start(), calls=%async_computation.8 | async-start | bytes 8912896 | tf_op jit(solution)/shard_map/reduce_scatter | solution.py:83
  174.0 285.5 %all-gather.22.cloned.1.call-start = ((), (), s32[]{:S(2)}) async-start(), calls=%async_computation.9 | async-start | bytes 3145728 | tf_op jit(solution)/shard_map/all_gather | solution.py:22
  426.6 161.5 %all-gather.24.cloned.1.call-start = ((), (), s32[]{:S(2)}) async-start(), calls=%async_computation.10 | async-start | bytes 17825792 | tf_op jit(solution)/shard_map/all_gather | solution.py:97
  427.4 266.4 %reduce-scatter.8.cloned.1.call-start = ((), (), s32[]{:S(2)}) async-start(), calls=%async_computation.13 | async-start | bytes 8912896 | tf_op jit(solution)/shard_map/reduce_scatter | solution.py:84
  435.2 292.8 %copy-start.2 = (f32[2,128,1024]{2,1,0:T(8,128)S(1)}, f32[2,128,1024]{2,1,0:T(8,128)}, u32[]{:S(2)}) copy-start(f32[2,128,1024]{2,1,0:T(8,128)} %get-tuple-element.11) | copy-start | bytes 3145732
  435.2 292.8 %all-gather.26.cloned.1.call-start = ((), (), s32[]{:S(2)}) async-start(), calls=%async_computation.11 | async-start | bytes 3145728 | tf_op jit(solution)/shard_map/all_gather | solution.py:22
  602.5 202.0 %all-gather.32.cloned.1.call-start = ((), (), s32[]{:S(2)}) async-start(), calls=%async_computation.15 | async-start | bytes 8912896 | tf_op jit(solution)/shard_map/all_gather | solution.py:29
  693.9 131.9 %all-gather.28.cloned.1.call-start = ((), (), s32[]{:S(2)}) async-start(), calls=%async_computation.12 | async-start | bytes 1572864 | tf_op jit(solution)/shard_map/all_gather | solution.py:22
  742.8 189.9 %copy-start.4 = (f32[128,1024]{1,0:T(8,128)S(1)}, f32[128,1024]{1,0:T(8,128)}, u32[]{:S(2)}) copy-start(f32[128,1024]{1,0:T(8,128)} %reduce-scatter.8.cloned.1.call-done) | copy-start | bytes 1572868
  742.9 113.6 %all-gather.34.cloned.1.call-start = ((), (), s32[]{:S(2)}) async-start(), calls=%async_computation.16 | async-start | bytes 1572864 | tf_op jit(solution)/shard_map/all_gather | solution.py:22
  835.0 97.8 %all-gather.30.cloned.1.call-start = ((), (), s32[]{:S(2)}) async-start(), calls=%async_computation.14 | async-start | bytes 8912896 | tf_op jit(solution)/shard_map/all_gather | solution.py:29
  835.6 146.0 %copy-start.1 = (bf16[2,8,256,256]{3,2,1,0:T(8,128)(2,1)S(1)}, bf16[2,8,256,256]{3,2,1,0:T(8,128)(2,1)}, u32[]{:S(2)}) copy-start(bf16[2,8,256,256]{3,2,1,0:T(8,128)(2,1)} %param.9) | copy-start | bytes 6291460
Sparse Core Ops, SparseCore 0:
  8.9 35.8 all-gather.15
  46.9 52.4 all-gather.17
  100.9 31.2 all-gather.13
  133.7 33.0 all-gather.19
  170.7 103.4 reduce-scatter.3
  278.1 103.0 reduce-scatter.5
  426.8 32.6 all-gather.21
  461.6 126.4 all-gather.23
  592.2 101.6 reduce-scatter.7
  695.2 32.7 all-gather.25
  730.2 74.2 all-gather.31
  805.9 19.8 all-gather.27
  835.1 21.2 all-gather.33
  858.4 74.2 all-gather.29
where the time goes:
time: 989 us; the launch traced here: 988 us
  waiting for transfers between devices  804 us (81%)
  blocking collectives  79.6 us (8%)
  matrix products  71.7 us (7%)
  between operations  14.1 us (1%)
  other arithmetic  11.6 us (1%)
    all_gather x2, waiting for transfers between devices, panel_product(): lax.all_gather(right_block, 'dp', axis=1, tiled=True)  138 us
    all_gather x1, waiting for transfers between devices, per_device(): columns = lax.all_gather(iterate, 'dp', axis=1, tiled=True)  129 us
    reduce_scatter x1, waiting for transfers between devices, per_device(): lax.psum_scatter(g_part, 'dp', scatter_dimension=0, tiled=True)  107 us
    all_gather x4, waiting for transfers between devices, panel_rows(): return lax.all_gather(block, 'fac', axis=2, tiled=True)  100 us
    reduce_scatter x1, waiting for transfers between devices, per_device(): lax.psum_scatter(a_part, 'dp', scatter_dimension=0, tiled=True)  100 us
    reduce_scatter x1, waiting for transfers between devices, per_device(): lax.psum_scatter(grad_part, 'dp', scatter_dimension=0, tiled=True)  91.3 us
    all_gather x1, waiting for transfers between devices, per_device(): lax.all_gather(w_out, 'dp', axis=1, tiled=True)  54.7 us
    psum x1, blocking collectives, per_device(): lax.psum((jnp.sum(a_block * a_block), jnp.sum(g_block * g_block)), ('dp',...  40.5 us
  transfers between devices with their start and end apart: 14, of which 14 were waited for; matrix products, arithmetic and copies ran while one was open for 7% of the time, Pallas kernels for 0%

commit v1 on v0

--- a/solution.py
+++ b/solution.py
@@ -2,6 +2,7 @@
 import jax.numpy as jnp
 from jax import lax
 from jax.sharding import PartitionSpec as P
+from jax.lax import axis_index, axis_size, ppermute
 
 ORBS = 256
 NE = 48
@@ -9,6 +10,25 @@
 epsilon = 1e-06
 highest = lax.Precision.HIGHEST
 contract_first = (((0,), (0,)), ((), ()))
+
+
+def words_direct(frame_in, named_axis, array_dim, matrix):
+    tmp = axis_size(named_axis)
+    piece_next = axis_index(named_axis)
+    q_next, local_out, taken_in = (tmp, piece_next, frame_in.shape[array_dim])
+    so_far_all = [(j0, (j0 + 1) % q_next) for j0 in range(q_next)]
+    trail = [(j0, (j0 - 1) % q_next) for j0 in range(q_next)]
+    oldest = q_next // 2
+    high = last = frame_in
+    v_next = matrix(frame_in, local_out * taken_in)
+    for no in range(1, oldest + 1):
+        high = ppermute(high, named_axis, so_far_all)
+        if no < q_next - oldest:
+            last = ppermute(last, named_axis, trail)
+            v_next = v_next + matrix(last, (local_out + no) % q_next * taken_in)
+        spare = matrix(high, (local_out - no) % q_next * taken_in)
+        v_next = v_next + spare
+    return v_next
 
 
 def keep_mask(occupations):
@@ -23,11 +43,16 @@
 
 
 def panel_product(left_rows, right_block):
-    return jnp.einsum(
-        "brk,bkc->brc",
-        left_rows,
-        lax.all_gather(right_block, "dp", axis=1, tiled=True),
-        precision=highest,
+    return words_direct(
+        right_block,
+        "dp",
+        1,
+        lambda shard, at: jnp.einsum(
+            "brk,bkc->brc",
+            lax.dynamic_slice_in_dim(left_rows, at, shard.shape[1], axis=2),
+            shard,
+            precision=highest,
+        ),
     )
 
 

time: 989 us -> 923 us (0.933)
  waiting for transfers between devices: 804 us -> 602 us
  starting transfers between devices: 0.93 us -> 104 us
  matrix products: 71.7 us -> 91.1 us
    all_gather x2 -> x0, waiting for transfers between devices: 138 us -> none  [panel_product(): lax.all_gather(right_block, 'dp', axis=1, tiled=True)]
    ppermute x0 -> x30, starting transfers between devices: none -> 104 us  [the longest x16 58.7 us: words_direct(): high = ppermute(high, named_axis, so_far_all)]
    all_gather x4, waiting for transfers between devices: 100 us -> 32.1 us  [panel_rows(): return lax.all_gather(block, 'fac', axis=2, tiled=True)]
    ppermute x0 -> x30, waiting for transfers between devices: none -> 39.9 us  [the longest x16 31.1 us: words_direct(): high = ppermute(high, named_axis, so_far_all)]
    reduce_scatter x1, waiting for transfers between devices: 91.3 us -> 60.6 us  [per_device(): lax.psum_scatter(grad_part, 'dp', scatter_dimension=0, tiled=True)]
    dot_general x2 -> x32, matrix products: 17.3 us -> 36.3 us  [panel_product(): jnp.einsum('brk,bkc->brc', lax.dynamic_slice_in_dim(left_rows, at, shard....]
  transfers between devices with their start and end apart: 14 -> 42, of which waited for: 14 -> 20; matrix products, arithmetic and copies ran while one was open for 7% -> 11% of each run, Pallas kernels for 0% -> 0%
where the time goes in v1:
time: 923 us; the launch traced here: 914 us
  waiting for transfers between devices  602 us (65%)
  starting transfers between devices  104 us (11%)
  matrix products  91.1 us (10%)
  blocking collectives  86.7 us (9%)
  between operations  15.3 us (2%)
  other arithmetic  9.61 us (1%)
    all_gather x1, waiting for transfers between devices, per_device(): columns = lax.all_gather(iterate, 'dp', axis=1, tiled=True)  129 us
    reduce_scatter x1, waiting for transfers between devices, per_device(): lax.psum_scatter(g_part, 'dp', scatter_dimension=0, tiled=True)  107 us
    reduce_scatter x1, waiting for transfers between devices, per_device(): lax.psum_scatter(a_part, 'dp', scatter_dimension=0, tiled=True)  92 us
    reduce_scatter x1, waiting for transfers between devices, per_device(): lax.psum_scatter(grad_part, 'dp', scatter_dimension=0, tiled=True)  60.6 us
    ppermute x16, starting transfers between devices, words_direct(): high = ppermute(high, named_axis, so_far_all)  58.7 us
    all_gather x1, waiting for transfers between devices, per_device(): lax.all_gather(w_out, 'dp', axis=1, tiled=True)  54.7 us
    psum x1, blocking collectives, per_device(): inner_sum = lax.psum(jnp.sum(grad_block * pre), ('dp', 'fac'))  45.8 us
    ppermute x14, starting transfers between devices, words_direct(): last = ppermute(last, named_axis, trail)  44.9 us
  transfers between devices with their start and end apart: 42, of which 20 were waited for; matrix products, arithmetic and copies ran while one was open for 11% of the time, Pallas kernels for 0%

profile of v1, /device:TPU:0, one launch (start us, length us, event | category | flops | bytes accessed | tf_op | source)
XLA Modules:
  0.0 913.5 jit_solution(18093133252359987454)
XLA Ops:
  9.9 34.8 %all-gather.13.cloned.1.call-done = bf16[512,2048]{1,0:T(8,128)(2,1)} async-done(((bf16[512,1024]{1,0:T(8,128)(2,1)}), bf16[512,2048]{1,0:T(8,128)(2,1)}) %all-gather.13.cloned.1.call-update) | async-done | bytes 2097168 | tf_op jit(solution)/shard_map/all_gather | solution.py:72
  44.7 54.7 %all-gather.15.cloned.1.call-done = bf16[1024,2048]{1,0:T(8,128)(2,1)} async-done(((bf16[1024,128]{1,0:T(8,128)(2,1)}), bf16[1024,2048]{1,0:T(8,128)(2,1)}) %all-gather.15.cloned.1.call-update) | async-done | bytes 4194320 | tf_op jit(solution)/shard_map/all_gather | solution.py:82
  99.4 5.2 fusion.9
  107.5 24.8 %all-gather.11.cloned.1.call-done = bf16[512,2048]{1,0:T(8,128)(2,1)} async-done(((bf16[512,1024]{1,0:T(8,128)(2,1)}), bf16[512,2048]{1,0:T(8,128)(2,1)}) %all-gather.11.cloned.1.call-update) | async-done | bytes 2097168 | tf_op jit(solution)/shard_map/all_gather | solution.py:71
  132.3 2.2 fusion
  135.1 1.3 copy-done.4
  136.4 6.0 convolution_multiply_fusion.2
  142.4 24.4 %all-gather.17.cloned.1.call-done = bf16[512,2048]{1,0:T(8,128)(2,1)} async-done(((bf16[512,1024]{1,0:T(8,128)(2,1)}), bf16[512,2048]{1,0:T(8,128)(2,1)}) %all-gather.17.cloned.1.call-update) | async-done | bytes 2097168 | tf_op jit(solution)/shard_map/all_gather | solution.py:91
  166.8 7.3 convolution_multiply_fusion.1
  174.1 7.7 convolution_multiply_fusion
  182.2 92.0 %reduce-scatter.4.cloned.1.call-done = f32[128,1024]{1,0:T(8,128)} async-done(((f32[2048,1024]{1,0:T(8,128)}), f32[128,1024]{1,0:T(8,128)}) %reduce-scatter.4.cloned.1.call-update) | async-done | bytes 524304 | tf_op jit(solution)/shard_map/reduce_scatter | solution.py:107
  274.2 107.0 %reduce-scatter.6.cloned.1.call-done = f32[128,1024]{1,0:T(8,128)} async-done(((f32[2048,1024]{1,0:T(8,128)}), f32[128,1024]{1,0:T(8,128)}) %reduce-scatter.6.cloned.1.call-update) | async-done | bytes 524304 | tf_op jit(solution)/shard_map/reduce_scatter | solution.py:108
  381.2 2.1 multiply_reduce_fusion.2
  383.3 40.8 %all-reduce = (f32[1]{0:T(128)}, f32[1]{0:T(128)}) all-reduce(f32[1]{0:T(128)} %bitcast.2, f32[1]{0:T(128)} %bitcast), channel_id=1, replica_groups=mesh['dp'=16,'fac'=2] {'dp','fac'}, use_global_device_ids=true, to_apply=%region_8.9 | all-reduce | flops 2 | bytes 16 | tf_op jit(solution)/shard_map/psum | solution.py:116
  425.4 1.6 multiply_subtract_fusion
  427.8 60.6 %reduce-scatter.8.cloned.1.call-done = f32[128,1024]{1,0:T(8,128)} async-done(((f32[2048,1024]{1,0:T(8,128)}), f32[128,1024]{1,0:T(8,128)}) %reduce-scatter.8.cloned.1.call-update) | async-done | bytes 524304 | tf_op jit(solution)/shard_map/reduce_scatter | solution.py:109
  488.4 4.4 collective-permute-start
  492.9 7.2 collective-permute-done.1
  500.0 2.0 collective-permute-start.3
  502.0 20.7 %all-gather.19.cloned.1.call-done = f32[2,128,2048]{2,1,0:T(8,128)} async-done(((f32[2,128,1024]{2,1,0:T(8,128)}), f32[2,128,2048]{2,1,0:T(8,128)}) %all-gather.19.cloned.1.call-update) | async-done | bytes 2097168 | tf_op jit(solution)/shard_map/all_gather | solution.py:42
  522.7 128.7 %all-gather.21.cloned.1.call-done = f32[2,2048,1024]{2,1,0:T(8,128)} async-done(((f32[2,128,1024]{2,1,0:T(8,128)}), f32[2,2048,1024]{2,1,0:T(8,128)}) %all-gather.21.cloned.1.call-update) | async-done | bytes 16777232 | tf_op jit(solution)/shard_map/all_gather | solution.py:122
  651.4 14.4 %fusion.161 = f32[2,128,1024]{2,1,0:T(8,128)} fusion(f32[2,128,2048]{2,1,0:T(8,128)} %all-gather.19.cloned.1.call-done, f32[2,2048,1024]{2,1,0:T(8,128)} %all-gather.21.cloned.1.call-done), kind=kOutput, calls=%fused_computation.201 | convolution fusion | flops 6442450944 | bytes 19922944 | tf_op jit(solution)/shard_map/brk,bkc->brc/dot_general | solution.py:123
  667.1 6.7 collective-permute-done.2
  673.8 4.7 collective-permute-start.4
  678.5 6.7 collective-permute-start.7
  685.3 4.6 collective-permute-start.6
  690.0 8.9 collective-permute-start.9
  698.9 2.5 collective-permute-start.8
  701.5 9.7 %collective-permute-start.11 = (f32[1,128,1024]{2,1,0:T(8,128)}, f32[1,128,1024]{2,1,0:T(8,128)}, u32[]{:S(2)}, u32[]{:S(2)}) collective-permute-start(f32[1,128,1024]{2,1,0:T(8,128)} %collective-permute-done.9), channel_id=1, source_target_pairs={{0,2},{2,4},{4,6},{6,8},{8,10},{10,12},{12,14},{14,16},{16,18},{18... | collective-permute-start | bytes 1572872 | tf_op jit(solution)/shard_map/ppermute | solution.py:25
  711.2 13.7 %convolution_subtract_fusion = f32[2,128,1024]{2,1,0:T(8,128)S(1)} fusion(f32[2,128,2048]{2,1,0:T(8,128)} %all-gather.23.cloned.1.call-done, f32[2,2048,1024]{2,1,0:T(8,128)} %all-gather.21.cloned.1.call-done, f32[2,128,1024]{2,1,0:T(8,128)S(1)} %copy-done.2), kind=kOutput, calls=%fused_computation.14 | convolution fusion | flops 6442975232 | bytes 20971520 | tf_op jit(solution)/shard_map/brk,bkc->brc/dot_general | solution.py:124
  726.2 2.6 collective-permute-start.13
  728.8 1.7 collective-permute-start.16
  730.5 2.8 collective-permute-start.15
  733.3 4.6 collective-permute-start.12
  737.9 16.6 %collective-permute-start.14 = (f32[1,128,1024]{2,1,0:T(8,128)}, f32[1,128,1024]{2,1,0:T(8,128)}, u32[]{:S(2)}, u32[]{:S(2)}) collective-permute-start(f32[1,128,1024]{2,1,0:T(8,128)} %collective-permute-done.13), channel_id=1, source_target_pairs={{0,2},{2,4},{4,6},{6,8},{8,10},{10,12},{12,14},{14,16},{16,18},{18... | collective-permute-start | bytes 1572872 | tf_op jit(solution)/shard_map/ppermute | solution.py:25
  754.5 3.0 collective-permute-start.18
  757.5 1.7 collective-permute-start.17
  759.2 1.7 fusion.54
  760.9 1.7 fusion.57
  762.7 1.7 fusion.60
  769.2 1.6 fusion.20
  770.9 1.6 fusion.19
  772.5 1.6 fusion.51
  774.2 1.6 fusion.18
  775.8 2.4 convolution_add_fusion.9
  779.6 3.2 collective-permute-start.19
  782.8 7.3 collective-permute-done.20
  790.1 3.3 collective-permute-start.22
  794.5 11.4 %all-gather.27.cloned.1.call-done = f32[128,2048]{1,0:T(8,128)} async-done(((f32[128,1024]{1,0:T(8,128)}), f32[128,2048]{1,0:T(8,128)}) %all-gather.27.cloned.1.call-update) | async-done | bytes 1048592 | tf_op jit(solution)/shard_map/all_gather | solution.py:42
  805.9 1.7 fusion.40
  807.6 1.7 fusion.43
  810.2 1.6 convolution_add_fusion.8
  811.9 1.6 convolution_add_fusion.7
  813.5 4.5 collective-permute-start.23
  818.0 1.6 fusion.17
  819.6 1.6 fusion.16
  821.3 1.6 fusion.37
  824.7 4.7 collective-permute-start.25
  830.6 4.4 collective-permute-done.26
  836.1 4.7 collective-permute-start.27
  842.0 4.4 collective-permute-done.28
  846.4 2.4 collective-permute-start.29
  850.0 7.7 collective-permute-done.29
  858.9 45.8 %psum.23 = f32[]{:T(128)} all-reduce(f32[]{:T(128)} %get-tuple-element.15), channel_id=1, replica_groups=mesh['dp'=16,'fac'=2] {'dp','fac'}, use_global_device_ids=true, to_apply=%region_11.12 | all-reduce | flops 1 | bytes 8 | tf_op jit(solution)/shard_map/psum | solution.py:129
  (140 shorter events, 28.7 us)
Async XLA Ops:
  6.5 98.3 %copy-start = (bf16[2,8,256,256]{3,2,1,0:T(8,128)(2,1)S(1)}, bf16[2,8,256,256]{3,2,1,0:T(8,128)(2,1)}, u32[]{:S(2)}) copy-start(bf16[2,8,256,256]{3,2,1,0:T(8,128)(2,1)} %param.9) | copy-start | bytes 6291460
  6.5 2.3 copy-start.22
  6.5 38.2 %all-gather.13.cloned.1.call-start = ((), (), s32[]{:S(2)}) async-start(), calls=%async_computation.5 | async-start | bytes 3145728 | tf_op jit(solution)/shard_map/all_gather | solution.py:72
  7.3 92.1 %all-gather.15.cloned.1.call-start = ((), (), s32[]{:S(2)}) async-start(), calls=%async_computation.6 | async-start | bytes 4456448 | tf_op jit(solution)/shard_map/all_gather | solution.py:82
  8.0 124.2 %all-gather.11.cloned.1.call-start = ((), (), s32[]{:S(2)}) async-start(), calls=%async_computation.3 | async-start | bytes 3145728 | tf_op jit(solution)/shard_map/all_gather | solution.py:71
  8.7 158.0 %all-gather.17.cloned.1.call-start = ((), (), s32[]{:S(2)}) async-start(), calls=%async_computation.7 | async-start | bytes 3145728 | tf_op jit(solution)/shard_map/all_gather | solution.py:91
  107.4 27.1 %copy-start.21 = (f32[2048]{0:T(1024)S(1)}, f32[2048]{0:T(1024)}, u32[]{:S(2)}) copy-start(f32[2048]{0:T(1024)} %param.8) | copy-start | bytes 24580
  107.5 166.7 %reduce-scatter.4.cloned.1.call-start = ((), (), s32[]{:S(2)}) async-start(), calls=%async_computation.4 | async-start | bytes 8912896 | tf_op jit(solution)/shard_map/reduce_scatter | solution.py:107
  132.3 2.2 copy-start.3
  135.1 1.3 copy-start.4
  142.4 238.8 %reduce-scatter.6.cloned.1.call-start = ((), (), s32[]{:S(2)}) async-start(), calls=%async_computation.8 | async-start | bytes 8912896 | tf_op jit(solution)/shard_map/reduce_scatter | solution.py:108
  174.1 314.3 %reduce-scatter.8.cloned.1.call-start = ((), (), s32[]{:S(2)}) async-start(), calls=%async_computation.13 | async-start | bytes 8912896 | tf_op jit(solution)/shard_map/reduce_scatter | solution.py:109
  181.9 340.8 %all-gather.19.cloned.1.call-start = ((), (), s32[]{:S(2)}) async-start(), calls=%async_computation.9 | async-start | bytes 3145728 | tf_op jit(solution)/shard_map/all_gather | solution.py:42
  427.1 224.3 %all-gather.21.cloned.1.call-start = ((), (), s32[]{:S(2)}) async-start(), calls=%async_computation.10 | async-start | bytes 17825792 | tf_op jit(solution)/shard_map/all_gather | solution.py:122
  427.8 283.4 %all-gather.23.cloned.1.call-start = ((), (), s32[]{:S(2)}) async-start(), calls=%async_computation.11 | async-start | bytes 3145728 | tf_op jit(solution)/shard_map/all_gather | solution.py:42
  488.4 222.7 %copy-start.2 = (f32[2,128,1024]{2,1,0:T(8,128)S(1)}, f32[2,128,1024]{2,1,0:T(8,128)}, u32[]{:S(2)}) copy-start(f32[2,128,1024]{2,1,0:T(8,128)} %get-tuple-element.11) | copy-start | bytes 3145732
  488.4 11.6 %collective-permute-start.1 = (f32[1,128,1024]{2,1,0:T(8,128)}, f32[1,128,1024]{2,1,0:T(8,128)S(1)}, u32[]{:S(2)}, u32[]{:S(2)}) collective-permute-start(f32[1,128,1024]{2,1,0:T(8,128)} %bitcast.192), channel_id=1, source_target_pairs={{0,2},{2,4},{4,6},{6,8},{8,10},{10,12},{12,14},{14,16},{16,18},{18... | collective-permute-start | bytes 1572872 | tf_op jit(solution)/shard_map/ppermute | solution.py:25
  488.4 177.4 %collective-permute-start = (f32[1,128,1024]{2,1,0:T(8,128)}, f32[1,128,1024]{2,1,0:T(8,128)S(1)}, u32[]{:S(2)}, u32[]{:S(2)}) collective-permute-start(f32[1,128,1024]{2,1,0:T(8,128)} %bitcast.193), channel_id=1, source_target_pairs={{0,30},{2,0},{4,2},{6,4},{8,6},{10,8},{12,10},{14,12},{16,14},{18,... | collective-permute-start | bytes 1572872 | tf_op jit(solution)/shard_map/ppermute | solution.py:27
  500.0 165.7 %copy-start.12 = (f32[1,128,1024]{2,1,0:T(8,128)}, f32[1,128,1024]{2,1,0:T(8,128)S(1)}, u32[]{:S(2)}) copy-start(f32[1,128,1024]{2,1,0:T(8,128)S(1)} %collective-permute-done.1) | copy-start | bytes 1572868
  500.0 167.1 %collective-permute-start.3 = (f32[1,128,1024]{2,1,0:T(8,128)S(1)}, f32[1,128,1024]{2,1,0:T(8,128)S(1)}, u32[]{:S(2)}, u32[]{:S(2)}) collective-permute-start(f32[1,128,1024]{2,1,0:T(8,128)S(1)} %collective-permute-done.1), channel_id=1, source_target_pairs={{0,2},{2,4},{4,6},{6,8},{8,10},{10,12},{12,14},{14,16},{16,18},{18... | collective-permute-start | bytes 1572872 | tf_op jit(solution)/shard_map/ppermute | solution.py:25
  665.8 93.4 %all-gather.25.cloned.1.call-start = ((), (), s32[]{:S(2)}) async-start(), calls=%async_computation.12 | async-start | bytes 1572864 | tf_op jit(solution)/shard_map/all_gather | solution.py:42
  665.9 1.3 copy-start.14
  665.9 8.0 collective-permute-start.2
  667.1 44.0 %copy-start.16 = (f32[1,128,1024]{2,1,0:T(8,128)}, f32[1,128,1024]{2,1,0:T(8,128)S(1)}, u32[]{:S(2)}) copy-start(f32[1,128,1024]{2,1,0:T(8,128)S(1)} %collective-permute-done.3) | copy-start | bytes 1572868
  667.1 11.4 %collective-permute-start.5 = (f32[1,128,1024]{2,1,0:T(8,128)S(1)}, f32[1,128,1024]{2,1,0:T(8,128)S(1)}, u32[]{:S(2)}, u32[]{:S(2)}) collective-permute-start(f32[1,128,1024]{2,1,0:T(8,128)S(1)} %collective-permute-done.3), channel_id=1, source_target_pairs={{0,2},{2,4},{4,6},{6,8},{8,10},{10,12},{12,14},{14,16},{16,18},{18... | collective-permute-start | bytes 1572872 | tf_op jit(solution)/shard_map/ppermute | solution.py:25
  673.8 11.5 %collective-permute-start.4 = (f32[1,128,1024]{2,1,0:T(8,128)S(1)}, f32[1,128,1024]{2,1,0:T(8,128)S(1)}, u32[]{:S(2)}, u32[]{:S(2)}) collective-permute-start(f32[1,128,1024]{2,1,0:T(8,128)S(1)} %collective-permute-done.2), channel_id=1, source_target_pairs={{0,30},{2,0},{4,2},{6,4},{8,6},{10,8},{12,10},{14,12},{16,14},{18,... | collective-permute-start | bytes 1572872 | tf_op jit(solution)/shard_map/ppermute | solution.py:27
  678.5 20.3 %copy-start.18 = (f32[1,128,1024]{2,1,0:T(8,128)}, f32[1,128,1024]{2,1,0:T(8,128)S(1)}, u32[]{:S(2)}) copy-start(f32[1,128,1024]{2,1,0:T(8,128)S(1)} %collective-permute-done.5) | copy-start | bytes 1572868
  678.5 11.4 %collective-permute-start.7 = (f32[1,128,1024]{2,1,0:T(8,128)S(1)}, f32[1,128,1024]{2,1,0:T(8,128)S(1)}, u32[]{:S(2)}, u32[]{:S(2)}) collective-permute-start(f32[1,128,1024]{2,1,0:T(8,128)S(1)} %collective-permute-done.5), channel_id=1, source_target_pairs={{0,2},{2,4},{4,6},{6,8},{8,10},{10,12},{12,14},{14,16},{16,18},{18... | collective-permute-start | bytes 1572872 | tf_op jit(solution)/shard_map/ppermute | solution.py:25
  685.3 25.9 %copy-start.8 = (f32[1,128,1024]{2,1,0:T(8,128)}, f32[1,128,1024]{2,1,0:T(8,128)S(1)}, u32[]{:S(2)}) copy-start(f32[1,128,1024]{2,1,0:T(8,128)S(1)} %collective-permute-done.4) | copy-start | bytes 1572868
  685.3 13.6 %collective-permute-start.6 = (f32[1,128,1024]{2,1,0:T(8,128)S(1)}, f32[1,128,1024]{2,1,0:T(8,128)S(1)}, u32[]{:S(2)}, u32[]{:S(2)}) collective-permute-start(f32[1,128,1024]{2,1,0:T(8,128)S(1)} %collective-permute-done.4), channel_id=1, source_target_pairs={{0,30},{2,0},{4,2},{6,4},{8,6},{10,8},{12,10},{14,12},{16,14},{18,... | collective-permute-start | bytes 1572872 | tf_op jit(solution)/shard_map/ppermute | solution.py:27
  689.9 11.4 %copy-start.20 = (f32[1,128,1024]{2,1,0:T(8,128)}, f32[1,128,1024]{2,1,0:T(8,128)S(1)}, u32[]{:S(2)}) copy-start(f32[1,128,1024]{2,1,0:T(8,128)S(1)} %collective-permute-done.7) | copy-start | bytes 1572868
  690.0 11.5 %collective-permute-start.9 = (f32[1,128,1024]{2,1,0:T(8,128)S(1)}, f32[1,128,1024]{2,1,0:T(8,128)}, u32[]{:S(2)}, u32[]{:S(2)}) collective-permute-start(f32[1,128,1024]{2,1,0:T(8,128)S(1)} %collective-permute-done.7), channel_id=1, source_target_pairs={{0,2},{2,4},{4,6},{6,8},{8,10},{10,12},{12,14},{14,16},{16,18},{18... | collective-permute-start | bytes 1572872 | tf_op jit(solution)/shard_map/ppermute | solution.py:25
  698.9 26.0 %copy-start.10 = (f32[1,128,1024]{2,1,0:T(8,128)}, f32[1,128,1024]{2,1,0:T(8,128)S(1)}, u32[]{:S(2)}) copy-start(f32[1,128,1024]{2,1,0:T(8,128)S(1)} %collective-permute-done.6) | copy-start | bytes 1572868
  698.9 27.2 %collective-permute-start.8 = (f32[1,128,1024]{2,1,0:T(8,128)S(1)}, f32[1,128,1024]{2,1,0:T(8,128)}, u32[]{:S(2)}, u32[]{:S(2)}) collective-permute-start(f32[1,128,1024]{2,1,0:T(8,128)S(1)} %collective-permute-done.6), channel_id=1, source_target_pairs={{0,30},{2,0},{4,2},{6,4},{8,6},{10,8},{12,10},{14,12},{16,14},{18,... | collective-permute-start | bytes 1572872 | tf_op jit(solution)/shard_map/ppermute | solution.py:27
  701.5 24.7 %collective-permute-start.11 = (f32[1,128,1024]{2,1,0:T(8,128)}, f32[1,128,1024]{2,1,0:T(8,128)}, u32[]{:S(2)}, u32[]{:S(2)}) collective-permute-start(f32[1,128,1024]{2,1,0:T(8,128)} %collective-permute-done.9), channel_id=1, source_target_pairs={{0,2},{2,4},{4,6},{6,8},{8,10},{10,12},{12,14},{14,16},{16,18},{18... | collective-permute-start | bytes 1572872 | tf_op jit(solution)/shard_map/ppermute | solution.py:25
  726.0 38.3 %copy-start.19 = (f32[1,128,1024]{2,1,0:T(8,128)S(1)}, f32[1,128,1024]{2,1,0:T(8,128)}, u32[]{:S(2)}) copy-start(f32[1,128,1024]{2,1,0:T(8,128)} %copy-done.18) | copy-start | bytes 1572868
  726.0 79.9 %all-gather.27.cloned.1.call-start = ((), (), s32[]{:S(2)}) async-start(), calls=%async_computation.14 | async-start | bytes 1572864 | tf_op jit(solution)/shard_map/all_gather | solution.py:42
  726.1 7.2 collective-permute-start.10
  726.2 11.8 %collective-permute-start.13 = (f32[1,128,1024]{2,1,0:T(8,128)}, f32[1,128,1024]{2,1,0:T(8,128)}, u32[]{:S(2)}, u32[]{:S(2)}) collective-permute-start(f32[1,128,1024]{2,1,0:T(8,128)} %collective-permute-done.11), channel_id=1, source_target_pairs={{0,2},{2,4},{4,6},{6,8},{8,10},{10,12},{12,14},{14,16},{16,18},{18... | collective-permute-start | bytes 1572872 | tf_op jit(solution)/shard_map/ppermute | solution.py:25
  728.8 25.7 %collective-permute-start.16 = (f32[1,128,1024]{2,1,0:T(8,128)}, f32[1,128,1024]{2,1,0:T(8,128)}, u32[]{:S(2)}, u32[]{:S(2)}) collective-permute-start(f32[1,128,1024]{2,1,0:T(8,128)} %get-tuple-element.10), channel_id=1, source_target_pairs={{0,2},{2,4},{4,6},{6,8},{8,10},{10,12},{12,14},{14,16},{16,18},{18... | collective-permute-start | bytes 1572872 | tf_op jit(solution)/shard_map/ppermute | solution.py:25
  730.5 27.0 %collective-permute-start.15 = (f32[1,128,1024]{2,1,0:T(8,128)}, f32[1,128,1024]{2,1,0:T(8,128)}, u32[]{:S(2)}, u32[]{:S(2)}) collective-permute-start(f32[1,128,1024]{2,1,0:T(8,128)} %get-tuple-element.10), channel_id=1, source_target_pairs={{0,30},{2,0},{4,2},{6,4},{8,6},{10,8},{12,10},{14,12},{16,14},{18,... | collective-permute-start | bytes 1572872 | tf_op jit(solution)/shard_map/ppermute | solution.py:27
  733.2 31.7 %copy-start.17 = (f32[1,128,1024]{2,1,0:T(8,128)S(1)}, f32[1,128,1024]{2,1,0:T(8,128)}, u32[]{:S(2)}) copy-start(f32[1,128,1024]{2,1,0:T(8,128)} %copy-done.16) | copy-start | bytes 1572868
  733.3 40.9 %collective-permute-start.12 = (f32[1,128,1024]{2,1,0:T(8,128)}, f32[1,128,1024]{2,1,0:T(8,128)}, u32[]{:S(2)}, u32[]{:S(2)}) collective-permute-start(f32[1,128,1024]{2,1,0:T(8,128)} %collective-permute-done.10), channel_id=1, source_target_pairs={{0,30},{2,0},{4,2},{6,4},{8,6},{10,8},{12,10},{14,12},{16,14},{18,... | collective-permute-start | bytes 1572872 | tf_op jit(solution)/shard_map/ppermute | solution.py:27
  737.9 37.9 %collective-permute-start.14 = (f32[1,128,1024]{2,1,0:T(8,128)}, f32[1,128,1024]{2,1,0:T(8,128)}, u32[]{:S(2)}, u32[]{:S(2)}) collective-permute-start(f32[1,128,1024]{2,1,0:T(8,128)} %collective-permute-done.13), channel_id=1, source_target_pairs={{0,2},{2,4},{4,6},{6,8},{8,10},{10,12},{12,14},{14,16},{16,18},{18... | collective-permute-start | bytes 1572872 | tf_op jit(solution)/shard_map/ppermute | solution.py:25
  754.5 23.8 %collective-permute-start.18 = (f32[1,128,1024]{2,1,0:T(8,128)}, f32[1,128,1024]{2,1,0:T(8,128)}, u32[]{:S(2)}, u32[]{:S(2)}) collective-permute-start(f32[1,128,1024]{2,1,0:T(8,128)} %collective-permute-done.16), channel_id=1, source_target_pairs={{0,2},{2,4},{4,6},{6,8},{8,10},{10,12},{12,14},{14,16},{16,18},{18... | collective-permute-start | bytes 1572872 | tf_op jit(solution)/shard_map/ppermute | solution.py:25
  757.5 22.1 %collective-permute-start.17 = (f32[1,128,1024]{2,1,0:T(8,128)}, f32[1,128,1024]{2,1,0:T(8,128)}, u32[]{:S(2)}, u32[]{:S(2)}) collective-permute-start(f32[1,128,1024]{2,1,0:T(8,128)} %collective-permute-done.15), channel_id=1, source_target_pairs={{0,30},{2,0},{4,2},{6,4},{8,6},{10,8},{12,10},{14,12},{16,14},{18,... | collective-permute-start | bytes 1572872 | tf_op jit(solution)/shard_map/ppermute | solution.py:27
  759.2 3.5 copy-start.6
  760.9 4.6 copy-start.5
  762.6 3.5 copy-start.15
  764.9 1.8 copy-start.13
  767.4 1.2 copy-start.11
  778.3 11.8 %collective-permute-start.20 = (f32[1,128,1024]{2,1,0:T(8,128)}, f32[1,128,1024]{2,1,0:T(8,128)}, u32[]{:S(2)}, u32[]{:S(2)}) collective-permute-start(f32[1,128,1024]{2,1,0:T(8,128)} %collective-permute-done.18), channel_id=1, source_target_pairs={{0,2},{2,4},{4,6},{6,8},{8,10},{10,12},{12,14},{14,16},{16,18},{18... | collective-permute-start | bytes 1572872 | tf_op jit(solution)/shard_map/ppermute | solution.py:25
  779.6 13.8 %collective-permute-start.19 = (f32[1,128,1024]{2,1,0:T(8,128)}, f32[1,128,1024]{2,1,0:T(8,128)}, u32[]{:S(2)}, u32[]{:S(2)}) collective-permute-start(f32[1,128,1024]{2,1,0:T(8,128)} %collective-permute-done.17), channel_id=1, source_target_pairs={{0,30},{2,0},{4,2},{6,4},{8,6},{10,8},{12,10},{14,12},{16,14},{18,... | collective-permute-start | bytes 1572872 | tf_op jit(solution)/shard_map/ppermute | solution.py:27
  790.1 19.9 %collective-permute-start.22 = (f32[1,128,1024]{2,1,0:T(8,128)}, f32[1,128,1024]{2,1,0:T(8,128)}, u32[]{:S(2)}, u32[]{:S(2)}) collective-permute-start(f32[1,128,1024]{2,1,0:T(8,128)} %collective-permute-done.20), channel_id=1, source_target_pairs={{0,2},{2,4},{4,6},{6,8},{8,10},{10,12},{12,14},{14,16},{16,18},{18... | collective-permute-start | bytes 1572872 | tf_op jit(solution)/shard_map/ppermute | solution.py:25
  793.3 20.2 %collective-permute-start.21 = (f32[1,128,1024]{2,1,0:T(8,128)}, f32[1,128,1024]{2,1,0:T(8,128)S(1)}, u32[]{:S(2)}, u32[]{:S(2)}) collective-permute-start(f32[1,128,1024]{2,1,0:T(8,128)} %collective-permute-done.19), channel_id=1, source_target_pairs={{0,30},{2,0},{4,2},{6,4},{8,6},{10,8},{12,10},{14,12},{16,14},{18,... | collective-permute-start | bytes 1572872 | tf_op jit(solution)/shard_map/ppermute | solution.py:27
  805.9 3.4 copy-start.7
  809.9 13.6 %collective-permute-start.24 = (f32[1,128,1024]{2,1,0:T(8,128)}, f32[1,128,1024]{2,1,0:T(8,128)S(1)}, u32[]{:S(2)}, u32[]{:S(2)}) collective-permute-start(f32[1,128,1024]{2,1,0:T(8,128)} %collective-permute-done.22), channel_id=1, source_target_pairs={{0,2},{2,4},{4,6},{6,8},{8,10},{10,12},{12,14},{14,16},{16,18},{18... | collective-permute-start | bytes 1572872 | tf_op jit(solution)/shard_map/ppermute | solution.py:25
  813.5 11.2 %collective-permute-start.23 = (f32[1,128,1024]{2,1,0:T(8,128)S(1)}, f32[1,128,1024]{2,1,0:T(8,128)S(1)}, u32[]{:S(2)}, u32[]{:S(2)}) collective-permute-start(f32[1,128,1024]{2,1,0:T(8,128)S(1)} %collective-permute-done.21), channel_id=1, source_target_pairs={{0,30},{2,0},{4,2},{6,4},{8,6},{10,8},{12,10},{14,12},{16,14},{18,... | collective-permute-start | bytes 1572872 | tf_op jit(solution)/shard_map/ppermute | solution.py:27
  823.5 11.5 %collective-permute-start.26 = (f32[1,128,1024]{2,1,0:T(8,128)S(1)}, f32[1,128,1024]{2,1,0:T(8,128)S(1)}, u32[]{:S(2)}, u32[]{:S(2)}) collective-permute-start(f32[1,128,1024]{2,1,0:T(8,128)S(1)} %collective-permute-done.24), channel_id=1, source_target_pairs={{0,2},{2,4},{4,6},{6,8},{8,10},{10,12},{12,14},{14,16},{16,18},{18... | collective-permute-start | bytes 1572872 | tf_op jit(solution)/shard_map/ppermute | solution.py:25
  824.7 11.4 %collective-permute-start.25 = (f32[1,128,1024]{2,1,0:T(8,128)S(1)}, f32[1,128,1024]{2,1,0:T(8,128)S(1)}, u32[]{:S(2)}, u32[]{:S(2)}) collective-permute-start(f32[1,128,1024]{2,1,0:T(8,128)S(1)} %collective-permute-done.23), channel_id=1, source_target_pairs={{0,30},{2,0},{4,2},{6,4},{8,6},{10,8},{12,10},{14,12},{16,14},{18,... | collective-permute-start | bytes 1572872 | tf_op jit(solution)/shard_map/ppermute | solution.py:27
  835.0 11.4 %collective-permute-start.28 = (f32[1,128,1024]{2,1,0:T(8,128)S(1)}, f32[1,128,1024]{2,1,0:T(8,128)S(1)}, u32[]{:S(2)}, u32[]{:S(2)}) collective-permute-start(f32[1,128,1024]{2,1,0:T(8,128)S(1)} %collective-permute-done.26), channel_id=1, source_target_pairs={{0,2},{2,4},{4,6},{6,8},{8,10},{10,12},{12,14},{14,16},{16,18},{18... | collective-permute-start | bytes 1572872 | tf_op jit(solution)/shard_map/ppermute | solution.py:25
  836.1 13.3 %collective-permute-start.27 = (f32[1,128,1024]{2,1,0:T(8,128)S(1)}, f32[1,128,1024]{2,1,0:T(8,128)S(1)}, u32[]{:S(2)}, u32[]{:S(2)}) collective-permute-start(f32[1,128,1024]{2,1,0:T(8,128)S(1)} %collective-permute-done.25), channel_id=1, source_target_pairs={{0,30},{2,0},{4,2},{6,4},{8,6},{10,8},{12,10},{14,12},{16,14},{18,... | collective-permute-start | bytes 1572872 | tf_op jit(solution)/shard_map/ppermute | solution.py:27
  846.4 11.3 %collective-permute-start.29 = (f32[1,128,1024]{2,1,0:T(8,128)S(1)}, f32[1,128,1024]{2,1,0:T(8,128)S(1)}, u32[]{:S(2)}, u32[]{:S(2)}) collective-permute-start(f32[1,128,1024]{2,1,0:T(8,128)S(1)} %collective-permute-done.28), channel_id=1, source_target_pairs={{0,2},{2,4},{4,6},{6,8},{8,10},{10,12},{12,14},{14,16},{16,18},{18... | collective-permute-start | bytes 1572872 | tf_op jit(solution)/shard_map/ppermute | solution.py:25
  849.4 56.9 %copy-start.1 = (bf16[2,8,256,256]{3,2,1,0:T(8,128)(2,1)S(1)}, bf16[2,8,256,256]{3,2,1,0:T(8,128)(2,1)}, u32[]{:S(2)}) copy-start(bf16[2,8,256,256]{3,2,1,0:T(8,128)(2,1)} %param.9) | copy-start | bytes 6291460
  (1 other events, 1.2 us)
Sparse Core Ops, SparseCore 0:
  8.9 35.8 all-gather.12
  46.9 52.4 all-gather.14
  101.0 31.2 all-gather.10
  133.7 33.0 all-gather.16
  170.7 103.4 reduce-scatter.3
  278.1 103.0 reduce-scatter.5
  385.3 103.0 reduce-scatter.7
  490.0 32.7 all-gather.18
  524.9 126.4 all-gather.20
  665.9 31.2 all-gather.22
  726.1 23.6 all-gather.24
  778.4 27.4 all-gather.26
